TPU v7x, 128 devices: a whole 4x4x4 slice. The times are simulated.
128 devices in a mesh: row: 16 (over z, y), col: 8 (over x, core).
Axes of the slice: x: 4, y: 4, z: 4, core: 2. Of those that a mesh axis runs over, the one named last changes fastest.
Arguments:
- covariance: float32 [4, 16, 256, 8, 8, 256], P(None, 'row', None, None, 'col'), as said below
- check_weights: float32 [4, 16, 256], P(None, 'row'), may hold values from 0.05 to 0.5
Outputs:
- trailing: float32 [4, 16, 256, 8, 8, 256], P(None, 'row', None, None, 'col')
- panels: float32 [4, 16, 256, 512], P(None, 'row')
- checksum: float32 [8, 8, 256], P(None, 'col')
Inputs may be any that keep to these rules, and one draw needn't show every extreme that they name: covariance is symmetric with smallest eigenvalue at least 0.5: an exponential kernel of jittered grid sites plus a nugget plus a small symmetric rough part.
All inputs are finite; a program needn't handle non-finite values.
Results may differ from a plain program's by a relative error of at most 0.0003.
Values sent between devices are 32-bit elements; how exact they have to be, the bound alone decides.
No kernel may reach another device: no remote copies, remote signals or barrier semaphores. Data moves between devices by JAX's collectives and lax.ppermute only.
A program may use at most 128 MiB of HBM per device.

v0:
```python
import jax
import jax.numpy as jnp
from jax import lax
from jax.sharding import PartitionSpec as P

HIGHEST = lax.Precision.HIGHEST


def from_root(value, axis, source):
    kept = jnp.where(lax.axis_index(axis) == source, value, 0).astype(value.dtype)
    return lax.psum(kept, axis)


def shards(covariance, check_weights):
    rows_size = lax.axis_size("row")
    cols_size = lax.axis_size("col")
    row_tiles = covariance.shape[0]
    width = covariance.shape[2]
    col_tiles = covariance.shape[3]
    matrix = covariance.reshape(row_tiles, width, col_tiles, width)
    row_index = lax.axis_index("row")
    col_index = lax.axis_index("col")
    global_rows = jnp.arange(row_tiles, dtype=jnp.int32) * rows_size + row_index
    global_cols = jnp.arange(col_tiles, dtype=jnp.int32) * cols_size + col_index
    panel_list = []
    for step in range(2):
        corner = matrix[step // rows_size, :, step // cols_size, :]
        corner = from_root(corner, "row", step % rows_size)
        corner = jnp.where(col_index == step % cols_size, corner, jnp.eye(width, dtype=jnp.float32))
        factor = jnp.linalg.cholesky(corner)
        column = matrix[:, :, step // cols_size, :].reshape(row_tiles * width, width)
        solved = jax.scipy.linalg.solve_triangular(factor, column.T, lower=True).T
        solved = solved.reshape(row_tiles, width, width)
        solved = jnp.where((global_rows >= step)[:, None, None], solved, 0.0)
        solved = from_root(solved, "col", step % cols_size)
        whole = lax.all_gather(solved, "row", axis=0, tiled=True)
        picked = global_cols % rows_size * row_tiles + global_cols // rows_size
        across = jnp.take(whole, picked, axis=0)
        matrix = matrix - jnp.einsum("iak,jbk->iajb", solved, across, precision=HIGHEST)
        panel_list.append(solved)
    keep = (global_rows >= 2)[:, None, None, None] & (global_cols >= 2)[None, None, :, None]
    trailing = jnp.where(keep, matrix, 0.0)
    weights = check_weights.reshape(row_tiles, width)
    partial_sums = jnp.einsum("ia,iajb->jb", weights, trailing, precision=HIGHEST)
    checksum = lax.psum(partial_sums, "row")
    panels = jnp.concatenate(panel_list, axis=2)
    return (
        trailing.reshape(row_tiles, 1, width, col_tiles, 1, width),
        panels.reshape(row_tiles, 1, width, 2 * width),
        checksum.reshape(col_tiles, 1, width),
    )


def solution(mesh):
    in_specs = (P(None, "row", None, None, "col", None), P(None, "row", None))
    out_specs = (
        P(None, "row", None, None, "col", None),
        P(None, "row", None, None),
        P(None, "col", None),
    )
    return jax.shard_map(shards, mesh=mesh, in_specs=in_specs, out_specs=out_specs, check_vma=False)
```

profile of v0, /device:TPU:0, one launch (start us, length us, event | category | flops | bytes accessed | tf_op | source)
XLA Modules:
  0.0 790.6 jit_solution(16580449472333877571)
XLA Ops:
  7.2 20.6 %copy.25 = f32[4,1,256,8,1,256]{2,5,3,0,4,1:T(8,128)} copy(f32[4,1,256,8,1,256]{5,4,3,2,1,0:T(1,128)} %param.7) | data formatting | bytes 16777216 | tf_op args[0]
  27.8 1.7 fusion.15
  29.5 1.3 slice.67
  31.5 85.0 %all-reduce.6.cloned.1.call-done = f32[256,256]{0,1:T(8,128)} async-done(((f32[256,256]{0,1:T(8,128)}), f32[256,256]{0,1:T(8,128)}) %all-reduce.6.cloned.1.call-update) | async-done | bytes 262160 | tf_op jit(solution)/shard_map/psum | solution.py:11
  118.7 11.7 %cholesky.130 = f32[128,128]{1,0:T(8,128)S(1)} custom-call(f32[128,128]{1,0:T(8,128)S(1)} %cholesky.194), custom_call_target="Cholesky" | custom-call | tf_op jit(solution)/shard_map/jit(cholesky)/cholesky | solution.py:30
  130.4 9.8 %custom-call.13 = f32[1,128,128]{1,2,0:T(8,128)S(1)} custom-call(f32[1,128,128]{2,1,0:T(8,128)S(1)} %get-tuple-element.58), custom_call_target="InvertDiagBlocksLowerTriangular" | custom-call | tf_op jit(solution)/shard_map/jit(cholesky)/cholesky | solution.py:30
  140.8 11.7 %cholesky.147 = f32[128,128]{1,0:T(8,128)S(1)} custom-call(f32[128,128]{1,0:T(8,128)S(1)} %convolution_subtract_fusion.4), custom_call_target="Cholesky" | custom-call | tf_op jit(solution)/shard_map/jit(cholesky)/cholesky | solution.py:30
  154.7 4.6 while.4
  155.8 1.4 bitcast_dynamic-update-slice_fusion.4
  157.9 1.4 bitcast_dynamic-update-slice_fusion.4
  159.3 19.7 %custom-call.14 = f32[2,128,128]{1,2,0:T(8,128)S(1)} custom-call(f32[2,128,128]{2,1,0:T(8,128)S(1)} %get-tuple-element.20), custom_call_target="InvertDiagBlocksLowerTriangular" | custom-call | tf_op jit(solution)/shard_map/jit(_solve_triangular)/triangular_solve | solution.py:32
  182.5 59.7 %all-reduce.8.cloned.1.call-done = f32[4,256,256]{2,1,0:T(8,128)} async-done(((f32[4,256,256]{2,1,0:T(8,128)}), f32[4,256,256]{2,1,0:T(8,128)}) %all-reduce.8.cloned.1.call-update) | async-done | bytes 1048592 | tf_op jit(solution)/shard_map/psum | solution.py:11
  242.4 113.1 %all-gather.3.cloned.1.call-done = f32[64,256,256]{2,1,0:T(8,128)} async-done(((f32[4,256,256]{2,1,0:T(8,128)}), f32[64,256,256]{2,1,0:T(8,128)}) %all-gather.3.cloned.1.call-update) | async-done | bytes 16777232 | tf_op jit(solution)/shard_map/all_gather | solution.py:36
  355.4 7.8 gather_fusion
  363.2 9.6 %convolution_subtract_fusion = f32[4,256,8,256]{1,3,2,0:T(8,128)S(1)} fusion(f32[8,256,256]{2,1,0:T(8,128)} %gather_fusion, f32[4,256,256]{2,1,0:T(8,128)S(1)} %copy-done.3, pred[8]{0:T(512)(128)(4,1)S(1)} %compare_and_fusion, f32[4,1,256,8,1,256]{2,5,3,0,4,1:T(8,128)} %copy.25), kind=kOutput, calls=%fused_computation.7 | convolution fusion | flops 6445072384 | bytes 19922952 | tf_op jit(solution)/shard_map/iak,jbk->iajb/dot_general | solution.py:39
  372.8 3.4 copy-done.2
  378.8 82.3 %all-reduce.10.cloned.1.call-done = f32[256,256]{0,1:T(8,128)} async-done(((f32[256,256]{0,1:T(8,128)}), f32[256,256]{0,1:T(8,128)}) %all-reduce.10.cloned.1.call-update) | async-done | bytes 262160 | tf_op jit(solution)/shard_map/psum | solution.py:11
  461.4 11.7 %cholesky.164 = f32[128,128]{1,0:T(8,128)S(1)} custom-call(f32[128,128]{1,0:T(8,128)S(1)} %cholesky.197), custom_call_target="Cholesky" | custom-call | tf_op jit(solution)/shard_map/jit(cholesky)/cholesky | solution.py:30
  473.8 9.8 %custom-call.15 = f32[1,128,128]{1,2,0:T(8,128)S(1)} custom-call(f32[1,128,128]{2,1,0:T(8,128)S(1)} %get-tuple-element.54), custom_call_target="InvertDiagBlocksLowerTriangular" | custom-call | tf_op jit(solution)/shard_map/jit(cholesky)/cholesky | solution.py:30
  484.1 11.7 %cholesky.181 = f32[128,128]{1,0:T(8,128)S(1)} custom-call(f32[128,128]{1,0:T(8,128)S(1)} %convolution_subtract_fusion.3), custom_call_target="Cholesky" | custom-call | tf_op jit(solution)/shard_map/jit(cholesky)/cholesky | solution.py:30
  498.0 4.3 while.5
  498.8 1.4 bitcast_dynamic-update-slice_fusion.5
  500.9 1.4 bitcast_dynamic-update-slice_fusion.5
  502.3 19.7 %custom-call.16 = f32[2,128,128]{1,2,0:T(8,128)S(1)} custom-call(f32[2,128,128]{2,1,0:T(8,128)S(1)} %get-tuple-element.21), custom_call_target="InvertDiagBlocksLowerTriangular" | custom-call | tf_op jit(solution)/shard_map/jit(_solve_triangular)/triangular_solve | solution.py:32
  525.5 61.7 %all-reduce.12.cloned.1.call-done = f32[4,256,256]{2,1,0:T(8,128)} async-done(((f32[4,256,256]{2,1,0:T(8,128)}), f32[4,256,256]{2,1,0:T(8,128)}) %all-reduce.12.cloned.1.call-update) | async-done | bytes 1048592 | tf_op jit(solution)/shard_map/psum | solution.py:11
  587.3 2.8 maximum_bitcast_fusion
  590.1 109.9 %all-gather.5.cloned.1.call-done = f32[64,256,256]{2,1,0:T(8,128)} async-done(((f32[4,256,256]{2,1,0:T(8,128)}), f32[64,256,256]{2,1,0:T(8,128)}) %all-gather.5.cloned.1.call-update) | async-done | bytes 16777232 | tf_op jit(solution)/shard_map/all_gather | solution.py:36
  700.0 6.4 gather_fusion.1
  706.5 9.6 %subtract_select_fusion = f32[4,256,8,256]{1,3,2,0:T(8,128)S(1)} fusion(f32[4,256,8,256]{1,3,2,0:T(8,128)} %copy-done.2, pred[4,8]{1,0:T(4,128)(4,1)S(1)} %broadcast_and_fusion, f32[8,256,256]{2,1,0:T(8,128)S(1)} %gather_fusion.1, f32[4,256,256]{2,1,0:T(8,128)S(1)} %copy-done.4, pred[8]{0:T(512)(128)(4,1)S(1)} %compare_and_fusion), kind=kOutput, calls=%fused_computation.6 | convolution fusion | flops 6447169536 | bytes 19922984 | tf_op jit(solution)/shard_map/iak,jbk->iajb/dot_general | solution.py:39
  716.1 7.2 fusion.28
  723.3 39.5 %psum.39 = f32[8,1,256]{2,1,0:T(1,128)} all-reduce(f32[8,1,256]{2,1,0:T(1,128)S(1)} %reshape.113), channel_id=1, replica_groups=mesh['row'=16,'col'=8] {'row'}, use_global_device_ids=true, to_apply=%region_8.12 | all-reduce | flops 2048 | bytes 16384 | tf_op jit(solution)/shard_map/psum | solution.py:45
  762.9 20.5 %copy.36 = f32[4,1,256,8,1,256]{5,4,3,2,1,0:T(1,128)} copy(f32[4,1,256,8,1,256]{2,5,3,0,4,1:T(8,128)} %bitcast.106) | data formatting | bytes 16777216
  (85 shorter events, 18.7 us)
Async XLA Ops:
  7.2 708.9 %copy-start = (f32[4,1,256]{2,1,0:T(1,128)S(1)}, f32[4,1,256]{2,1,0:T(1,128)}, u32[]{:S(2)}) copy-start(f32[4,1,256]{2,1,0:T(1,128)} %param.8) | copy-start | bytes 12292
  7.2 109.4 %all-reduce.6.cloned.1.call-start = ((), (), s32[]{:S(2)}) async-start(), calls=%async_computation | async-start | bytes 524288 | tf_op jit(solution)/shard_map/psum | solution.py:11
  29.5 212.7 %all-reduce.8.cloned.1.call-start = ((), (), s32[]{:S(2)}) async-start(), calls=%async_computation.1 | async-start | bytes 2097152 | tf_op jit(solution)/shard_map/psum | solution.py:11
  182.5 173.0 %all-gather.3.cloned.1.call-start = ((), (), s32[]{:S(2)}) async-start(), calls=%async_computation.2 | async-start | bytes 17825792 | tf_op jit(solution)/shard_map/all_gather | solution.py:36
  242.2 218.9 %all-reduce.10.cloned.1.call-start = ((), (), s32[]{:S(2)}) async-start(), calls=%async_computation.3 | async-start | bytes 524288 | tf_op jit(solution)/shard_map/psum | solution.py:11
  242.4 120.8 %copy-start.3 = (f32[4,256,256]{2,1,0:T(8,128)S(1)}, f32[4,256,256]{2,1,0:T(8,128)}, u32[]{:S(2)}) copy-start(f32[4,256,256]{2,1,0:T(8,128)} %all-reduce.8.cloned.1.call-done) | copy-start | bytes 3145732
  372.8 3.4 copy-start.2
  376.9 1.2 slice-start
  377.0 210.2 %all-reduce.12.cloned.1.call-start = ((), (), s32[]{:S(2)}) async-start(), calls=%async_computation.4 | async-start | bytes 2097152 | tf_op jit(solution)/shard_map/psum | solution.py:11
  525.5 174.6 %all-gather.5.cloned.1.call-start = ((), (), s32[]{:S(2)}) async-start(), calls=%async_computation.5 | async-start | bytes 17825792 | tf_op jit(solution)/shard_map/all_gather | solution.py:36
  590.1 116.4 %copy-start.4 = (f32[4,256,256]{2,1,0:T(8,128)S(1)}, f32[4,256,256]{2,1,0:T(8,128)}, u32[]{:S(2)}) copy-start(f32[4,256,256]{2,1,0:T(8,128)} %all-reduce.12.cloned.1.call-done) | copy-start | bytes 3145732
  716.1 7.2 copy-start.1
Sparse Core Ops, SparseCore 0:
  29.6 86.9 all-reduce.5
  182.6 59.5 all-reduce.7
  244.6 110.7 all-gather.2
  377.1 84.0 all-reduce.9
  525.6 61.5 all-reduce.11
  589.2 110.7 all-gather.4
where the time goes:
time: 800 us; the launch traced here: 791 us
  waiting for transfers between devices  512 us (64%)
  other arithmetic  118 us (15%)
  local copies, waits for them, and re-layouts  71.5 us (9%)
  blocking collectives  39.5 us (5%)
  matrix products  31 us (4%)
  between operations  17.6 us (2%)
    psum x4, waiting for transfers between devices, from_root(): return lax.psum(kept, axis)  289 us
    all_gather x2, waiting for transfers between devices, shards(): whole = lax.all_gather(solved, 'row', axis=0, tiled=True)  223 us
    another operation x13, other arithmetic, shards(): factor = jnp.linalg.cholesky(corner)  68.7 us
    unnamed x12, local copies, waits for them, and re-layouts  44.5 us
    psum x1, blocking collectives, shards(): checksum = lax.psum(partial_sums, 'row')  39.5 us
    another operation x5, other arithmetic, shards(): solved = jax.scipy.linalg.solve_triangular(factor, column.T, lower=True).T  39.4 us
    dot_general x2, matrix products, shards(): jnp.einsum('iak,jbk->iajb', solved, across, precision=HIGHEST)  19.2 us
  transfers between devices with their start and end apart: 6, of which 6 were waited for; matrix products, arithmetic and copies ran while one was open for 1% of the time, Pallas kernels for 0%

commit v1 on v0

--- a/solution.py
+++ b/solution.py
@@ -33,7 +33,9 @@
         solved = solved.reshape(row_tiles, width, width)
         solved = jnp.where((global_rows >= step)[:, None, None], solved, 0.0)
         solved = from_root(solved, "col", step % cols_size)
-        whole = lax.all_gather(solved, "row", axis=0, tiled=True)
+        whole = jnp.concatenate(
+            lax.all_to_all(jnp.stack([solved] * lax.axis_size("row")), "row", 0, 0), axis=0
+        )
         picked = global_cols % rows_size * row_tiles + global_cols // rows_size
         across = jnp.take(whole, picked, axis=0)
         matrix = matrix - jnp.einsum("iak,jbk->iajb", solved, across, precision=HIGHEST)

time: 800 us -> 1110 us (1.39)
  waiting for transfers between devices: 512 us -> 779 us
  local copies, waits for them, and re-layouts: 71.5 us -> 89.2 us
  starting transfers between devices: 0.42 us -> 14.9 us
    all_to_all x0 -> x2, waiting for transfers between devices: none -> 482 us  [shards(): lax.all_to_all(jnp.stack([solved] * lax.axis_size('row')), 'row', 0, 0)]
    all_gather x2 -> x0, waiting for transfers between devices: 223 us -> none  [shards(): whole = lax.all_gather(solved, 'row', axis=0, tiled=True)]
    another operation x2, local copies, waits for them, and re-layouts: 0.66 us -> 18 us  [shards(): jnp.stack([solved] * lax.axis_size('row'))]
    all_to_all x0 -> x2, starting transfers between devices: none -> 14.6 us  [shards(): lax.all_to_all(jnp.stack([solved] * lax.axis_size('row')), 'row', 0, 0)]
    unnamed x12 -> x10, local copies, waits for them, and re-layouts: 44.5 us -> 44.5 us
  transfers between devices with their start and end apart: 6 -> 6, of which waited for: 6 -> 6; matrix products, arithmetic and copies ran while one was open for 1% -> 0% of each run, Pallas kernels for 0% -> 0%
where the time goes in v1:
time: 1110 us; the launch traced here: 1090 us
  waiting for transfers between devices  779 us (70%)
  other arithmetic  117 us (11%)
  local copies, waits for them, and re-layouts  89.2 us (8%)
  blocking collectives  37.5 us (3%)
  matrix products  36.3 us (3%)
  between operations  17.1 us (2%)
  starting transfers between devices  14.9 us (1%)
    all_to_all x2, waiting for transfers between devices, shards(): lax.all_to_all(jnp.stack([solved] * lax.axis_size('row')), 'row', 0, 0)  482 us
    psum x4, waiting for transfers between devices, from_root(): return lax.psum(kept, axis)  297 us
    another operation x13, other arithmetic, shards(): factor = jnp.linalg.cholesky(corner)  68.7 us
    unnamed x10, local copies, waits for them, and re-layouts  44.5 us
    another operation x5, other arithmetic, shards(): solved = jax.scipy.linalg.solve_triangular(factor, column.T, lower=True).T  39.4 us
    psum x1, blocking collectives, shards(): checksum = lax.psum(partial_sums, 'row')  37.5 us
  transfers between devices with their start and end apart: 6, of which 6 were waited for; matrix products, arithmetic and copies ran while one was open for 0% of the time, Pallas kernels for 0%

profile of v1, /device:TPU:0, one launch (start us, length us, event | category | flops | bytes accessed | tf_op | source)
XLA Modules:
  0.0 1091.5 jit_solution(9009056170017310148)
XLA Ops:
  7.2 20.6 %copy.14 = f32[4,1,256,8,1,256]{2,5,3,0,4,1:T(8,128)} copy(f32[4,1,256,8,1,256]{5,4,3,2,1,0:T(1,128)} %param.7) | data formatting | bytes 16777216 | tf_op args[0]
  27.8 1.7 fusion.15
  31.2 85.3 %all-reduce.6.cloned.1.call-done = f32[256,256]{0,1:T(8,128)} async-done(((f32[256,256]{0,1:T(8,128)}), f32[256,256]{0,1:T(8,128)}) %all-reduce.6.cloned.1.call-update) | async-done | bytes 262160 | tf_op jit(solution)/shard_map/psum | solution.py:11
  118.7 11.7 %cholesky.130 = f32[128,128]{1,0:T(8,128)S(1)} custom-call(f32[128,128]{1,0:T(8,128)S(1)} %cholesky.194), custom_call_target="Cholesky" | custom-call | tf_op jit(solution)/shard_map/jit(cholesky)/cholesky | solution.py:30
  130.5 9.8 custom-call.13
  140.8 11.7 %cholesky.147 = f32[128,128]{1,0:T(8,128)S(1)} custom-call(f32[128,128]{1,0:T(8,128)S(1)} %convolution_subtract_fusion.4), custom_call_target="Cholesky" | custom-call | tf_op jit(solution)/shard_map/jit(cholesky)/cholesky | solution.py:30
  154.7 4.6 while.4
  155.9 1.4 bitcast_dynamic-update-slice_fusion.4
  159.3 19.7 %custom-call.14 = f32[2,128,128]{1,2,0:T(8,128)S(1)} custom-call(f32[2,128,128]{2,1,0:T(8,128)S(1)} %get-tuple-element.20), custom_call_target="InvertDiagBlocksLowerTriangular" | custom-call | tf_op jit(solution)/shard_map/jit(_solve_triangular)/triangular_solve | solution.py:32
  183.0 59.8 %all-reduce.8.cloned.1.call-done = f32[4,256,256]{2,1,0:T(8,128)} async-done(((f32[4,256,256]{2,1,0:T(8,128)}), f32[4,256,256]{2,1,0:T(8,128)}) %all-reduce.8.cloned.1.call-update) | async-done | bytes 1048592 | tf_op jit(solution)/shard_map/psum | solution.py:11
  242.7 9.0 stack.4
  251.7 7.2 all-to-all-start
  259.0 241.6 %all-to-all-done = f32[16,4,256,256]{3,2,1,0:T(8,128)} async-done(((f32[16,4,256,256]{3,2,1,0:T(8,128)}), f32[16,4,256,256]{3,2,1,0:T(8,128)}, u32[]{:S(2)}, u32[]{:S(2)}) %all-to-all-start) | async-done | bytes 16777248 | tf_op jit(solution)/shard_map/all_to_all | solution.py:37
  500.6 6.4 gather_fusion
  507.1 9.3 convolution_subtract_fusion
  516.4 3.4 copy-done.1
  522.4 90.3 %all-reduce.10.cloned.1.call-done = f32[256,256]{0,1:T(8,128)} async-done(((f32[256,256]{0,1:T(8,128)}), f32[256,256]{0,1:T(8,128)}) %all-reduce.10.cloned.1.call-update) | async-done | bytes 262160 | tf_op jit(solution)/shard_map/psum | solution.py:11
  613.0 11.7 %cholesky.164 = f32[128,128]{1,0:T(8,128)S(1)} custom-call(f32[128,128]{1,0:T(8,128)S(1)} %cholesky.197), custom_call_target="Cholesky" | custom-call | tf_op jit(solution)/shard_map/jit(cholesky)/cholesky | solution.py:30
  624.8 9.8 custom-call.15
  635.1 11.7 %cholesky.181 = f32[128,128]{1,0:T(8,128)S(1)} custom-call(f32[128,128]{1,0:T(8,128)S(1)} %convolution_subtract_fusion.3), custom_call_target="Cholesky" | custom-call | tf_op jit(solution)/shard_map/jit(cholesky)/cholesky | solution.py:30
  649.6 4.3 while.5
  653.9 19.7 %custom-call.16 = f32[2,128,128]{1,2,0:T(8,128)S(1)} custom-call(f32[2,128,128]{2,1,0:T(8,128)S(1)} %get-tuple-element.21), custom_call_target="InvertDiagBlocksLowerTriangular" | custom-call | tf_op jit(solution)/shard_map/jit(_solve_triangular)/triangular_solve | solution.py:32
  677.5 61.7 %all-reduce.12.cloned.1.call-done = f32[4,256,256]{2,1,0:T(8,128)} async-done(((f32[4,256,256]{2,1,0:T(8,128)}), f32[4,256,256]{2,1,0:T(8,128)}) %all-reduce.12.cloned.1.call-update) | async-done | bytes 1048592 | tf_op jit(solution)/shard_map/psum | solution.py:11
  739.2 9.0 stack.5
  748.3 7.4 all-to-all-start.1
  755.8 1.6 maximum_bitcast_fusion
  757.4 240.0 %all-to-all-done.1 = f32[16,4,256,256]{3,2,1,0:T(8,128)} async-done(((f32[16,4,256,256]{3,2,1,0:T(8,128)}), f32[16,4,256,256]{3,2,1,0:T(8,128)}, u32[]{:S(2)}, u32[]{:S(2)}) %all-to-all-start.1) | async-done | bytes 16777248 | tf_op jit(solution)/shard_map/all_to_all | solution.py:37
  997.4 7.8 gather_fusion.1
  1005.2 12.1 %subtract_select_fusion = f32[4,256,8,256]{1,3,2,0:T(8,128)} fusion(f32[4,256,8,256]{1,3,2,0:T(8,128)} %copy-done.1, pred[4,8]{1,0:T(4,128)(4,1)S(1)} %broadcast_and_fusion, f32[8,256,256]{2,1,0:T(8,128)} %gather_fusion.1, f32[4,256,256]{2,1,0:T(8,128)S(1)} %copy-done.3, pred[8]{0:T(512)(128)(4,1)S(1)} %compare_and_fusion), kind=kOutput, calls=%fused_computation.6 | convolution fusion | flops 6447169536 | bytes 19922984 | tf_op jit(solution)/shard_map/iak,jbk->iajb/dot_general | solution.py:41
  1017.4 20.5 %copy.23 = f32[4,1,256,8,1,256]{5,4,3,2,1,0:T(1,128)} copy(f32[4,1,256,8,1,256]{2,5,3,0,4,1:T(8,128)} %bitcast.110) | data formatting | bytes 16777216
  1037.9 9.4 fusion.28
  1047.3 37.5 %psum.39 = f32[8,1,256]{2,1,0:T(1,128)} all-reduce(f32[8,1,256]{2,1,0:T(1,128)S(1)} %reshape.125), channel_id=1, replica_groups=mesh['row'=16,'col'=8] {'row'}, use_global_device_ids=true, to_apply=%region_8.12 | all-reduce | flops 2048 | bytes 16384 | tf_op jit(solution)/shard_map/psum | solution.py:47
  (80 shorter events, 24.7 us)
Async XLA Ops:
  7.2 1030.7 %copy-start = (f32[4,1,256]{2,1,0:T(1,128)S(1)}, f32[4,1,256]{2,1,0:T(1,128)}, u32[]{:S(2)}) copy-start(f32[4,1,256]{2,1,0:T(1,128)} %param.8) | copy-start | bytes 12292
  7.2 109.4 %all-reduce.6.cloned.1.call-start = ((), (), s32[]{:S(2)}) async-start(), calls=%async_computation.2 | async-start | bytes 524288 | tf_op jit(solution)/shard_map/psum | solution.py:11
  29.5 213.3 %all-reduce.8.cloned.1.call-start = ((), (), s32[]{:S(2)}) async-start(), calls=%async_computation.3 | async-start | bytes 2097152 | tf_op jit(solution)/shard_map/psum | solution.py:11
  251.7 255.3 %copy-start.2 = (f32[4,256,256]{2,1,0:T(8,128)S(1)}, f32[4,256,256]{2,1,0:T(8,128)}, u32[]{:S(2)}) copy-start(f32[4,256,256]{2,1,0:T(8,128)} %all-reduce.8.cloned.1.call-done) | copy-start | bytes 3145732
  251.7 248.8 %all-to-all-start = ((f32[16,4,256,256]{3,2,1,0:T(8,128)}), f32[16,4,256,256]{3,2,1,0:T(8,128)}, u32[]{:S(2)}, u32[]{:S(2)}) async-start(f32[16,4,256,256]{3,2,1,0:T(8,128)} %stack.4), calls=%async_computation | async-start | bytes 33554432 | tf_op jit(solution)/shard_map/all_to_all | solution.py:37
  258.9 353.8 %all-reduce.10.cloned.1.call-start = ((), (), s32[]{:S(2)}) async-start(), calls=%async_computation.4 | async-start | bytes 524288 | tf_op jit(solution)/shard_map/psum | solution.py:11
  516.4 3.4 copy-start.1
  520.5 218.7 %all-reduce.12.cloned.1.call-start = ((), (), s32[]{:S(2)}) async-start(), calls=%async_computation.5 | async-start | bytes 2097152 | tf_op jit(solution)/shard_map/psum | solution.py:11
  748.3 7.5 copy-start.3
  748.3 249.2 %all-to-all-start.1 = ((f32[16,4,256,256]{3,2,1,0:T(8,128)}), f32[16,4,256,256]{3,2,1,0:T(8,128)}, u32[]{:S(2)}, u32[]{:S(2)}) async-start(f32[16,4,256,256]{3,2,1,0:T(8,128)} %stack.5), calls=%async_computation.1 | async-start | bytes 33554432 | tf_op jit(solution)/shard_map/all_to_all | solution.py:37
Sparse Core Ops, SparseCore 0:
  29.6 86.9 all-reduce.5
  183.1 59.5 all-reduce.7
  520.6 92.0 all-reduce.9
  677.6 61.5 all-reduce.11
